TPU v7x, 32 devices: a whole 2x2x4 slice. The times are simulated.
32 devices in a mesh: section: 4 (over z), node: 4 (over x, core), local: 2 (over y).
Axes of the slice: x: 2, y: 2, z: 4, core: 2. Of those that a mesh axis runs over, the one named last changes fastest.
Arguments:
- section_inputs: bfloat16 [4, 8, 4, 196, 512], P('section', ('node', 'local')), may hold values from -6 to 6
- grad_in: bfloat16 [4, 8, 196, 512], P('section', ('node', 'local')), may hold values from -6 to 6
- loss_grad: bfloat16 [8, 3, 196, 512], P(('node', 'local')), may hold values from -6 to 6
- w_reduce: bfloat16 [4, 512, 256], P('section'), may hold values from -0.25 to 0.25
- w_spatial: bfloat16 [4, 2304, 256], P('section'), may hold values from -0.125 to 0.125
- w_expand: bfloat16 [4, 256, 512], P('section'), may hold values from -0.375 to 0.375
- err_reduce: bfloat16 [4, 8, 512, 256], P('section', ('node', 'local')), may hold values from -360 to 360
- err_spatial: bfloat16 [4, 8, 2304, 256], P('section', ('node', 'local')), may hold values from -360 to 360
- err_expand: bfloat16 [4, 8, 256, 512], P('section', ('node', 'local')), may hold values from -360 to 360
- prior_reduce: float32 [4, 32, 256], P('section'), may hold values from -6 to 6
- prior_spatial: float32 [4, 32, 256], P('section'), may hold values from -6 to 6
- prior_expand: float32 [4, 32, 512], P('section'), may hold values from -6 to 6
Outputs:
- leaving: bfloat16 [4, 8, 196, 512], P('section', ('node', 'local'))
- basis_reduce: float32 [4, 32, 512], P('section', None, ('node', 'local'))
- basis_spatial: float32 [4, 32, 2304], P('section', None, ('node', 'local'))
- basis_expand: float32 [4, 32, 256], P('section', None, ('node', 'local'))
- right_reduce: float32 [4, 32, 256], P('section', None, ('node', 'local'))
- right_spatial: float32 [4, 32, 256], P('section', None, ('node', 'local'))
- right_expand: float32 [4, 32, 512], P('section', None, ('node', 'local'))
All inputs are finite; a program needn't handle non-finite values.
Results may differ from a plain program's by a relative error of at most 0.0095.
Values may be sent and summed in bfloat16 or wider, within the bound.
No kernel may reach another device: no remote copies, remote signals or barrier semaphores. Data moves between devices by JAX's collectives and lax.ppermute only.
A program may use at most 128 MiB of HBM per device.

v0:
```python
import math
import jax
import jax.numpy as jnp
from jax import lax
from jax.sharding import PartitionSpec as P

SIDE = 14
precise = lax.Precision.HIGHEST


def shifted_2(block, axis, distance):
    devices = range(lax.axis_size(axis))
    route = [(i - distance, i) for i in devices if i - distance in devices]
    return lax.ppermute(block, axis, route)


def silu_slope(values):
    logistic = jax.nn.sigmoid(values)
    return logistic * (1.0 + values * (1.0 - logistic))


def tap_shift(values, row_step, col_step, image_side):
    pixels = values.shape[0]
    offset = row_step * image_side + col_step
    padded = jnp.pad(values, ((image_side + 1, image_side + 1), (0, 0)))
    moved = lax.slice_in_dim(
        padded, image_side + 1 + offset, image_side + 1 + offset + pixels, axis=0
    )
    column = lax.broadcasted_iota(jnp.int32, (pixels, 1), 0) % image_side + col_step
    inside = jnp.logical_and(column >= 0, column < image_side)
    return jnp.where(inside, moved, jnp.zeros_like(moved))


def inner_rows(left_operand, right_operand):
    return lax.dot_general(
        left_operand, right_operand, (((0,), (0,)), ((), ())), preferred_element_type=jnp.float32
    )


def inner_cols(left_operand, right_operand, accuracy=None):
    return lax.dot_general(
        left_operand,
        right_operand,
        (((1,), (1,)), ((), ())),
        precision=accuracy,
        preferred_element_type=jnp.float32,
    )


def block_backward(inputs, upstream, reduce_weight, spatial_weight, expand_weight, image_side):
    channels = reduce_weight.shape[1]
    pre_reduce = jnp.dot(inputs, reduce_weight, preferred_element_type=jnp.float32)
    hidden_one = jax.nn.silu(pre_reduce).astype(jnp.bfloat16)
    shifted = []
    pre_spatial = jnp.zeros((inputs.shape[0], channels), jnp.float32)
    for tap in range(9):
        moved = tap_shift(hidden_one, tap // 3 - 1, tap % 3 - 1, image_side)
        shifted.append(moved)
        pre_spatial = pre_spatial + jnp.dot(
            moved,
            spatial_weight[tap * channels : (tap + 1) * channels],
            preferred_element_type=jnp.float32,
        )
    hidden_two = jax.nn.silu(pre_spatial).astype(jnp.bfloat16)
    back_two = inner_cols(upstream, expand_weight)
    back_spatial = (back_two * silu_slope(pre_spatial)).astype(jnp.bfloat16)
    back_one = jnp.zeros((inputs.shape[0], channels), jnp.float32)
    for tap in range(9):
        tap_term = inner_cols(back_spatial, spatial_weight[tap * channels : (tap + 1) * channels])
        back_one = back_one + tap_shift(tap_term, 1 - tap // 3, 1 - tap % 3, image_side)
    back_reduce = (back_one * silu_slope(pre_reduce)).astype(jnp.bfloat16)
    leaving = (upstream.astype(jnp.float32) + inner_cols(back_reduce, reduce_weight)).astype(
        jnp.bfloat16
    )
    spatial_grad = jnp.concatenate(
        [inner_rows(shifted[tap], back_spatial) for tap in range(9)], axis=0
    )
    gradients = (inner_rows(inputs, back_reduce), spatial_grad, inner_rows(hidden_two, upstream))
    return (leaving, gradients)


def local(
    section_inputs,
    grad_in,
    loss_grad,
    w_reduce,
    w_spatial,
    w_expand,
    err_reduce,
    err_spatial,
    err_expand,
    prior_reduce,
    prior_spatial,
    prior_expand,
):
    image_side = SIDE
    weights = (w_reduce[0], w_spatial[0], w_expand[0])
    last_section = lax.axis_index("section") == lax.axis_size("section") - 1
    upstream = grad_in[0, 0]
    leaving = upstream
    totals = tuple((jnp.zeros(weights[member].shape, jnp.float32) for member in range(3)))
    for tick_index in range(section_inputs.shape[2]):
        if tick_index > 0:
            arrived = shifted_2(leaving, "section", -1)
            upstream = jnp.where(last_section, loss_grad[0, tick_index - 1], arrived)
        leaving, gradients = block_backward(
            section_inputs[0, 0, tick_index],
            upstream,
            weights[0],
            weights[1],
            weights[2],
            image_side,
        )
        totals = tuple((totals[member] + gradients[member] for member in range(3)))
    errors = (err_reduce[0, 0], err_spatial[0, 0], err_expand[0, 0])
    matrices = tuple((totals[member] + errors[member].astype(jnp.float32) for member in range(3)))
    priors = (prior_reduce[0], prior_spatial[0], prior_expand[0])
    factors = tuple((inner_cols(priors[member], matrices[member], precise) for member in range(3)))
    replicas = lax.axis_size(("node", "local"))
    replica_index = lax.axis_index(("node", "local"))
    basis_list = []
    summed = lax.psum((factors[0], factors[1], factors[2]), ("node", "local"))
    partial_rights = []
    for member in range(3):
        triangle = jnp.linalg.cholesky(inner_cols(summed[member], summed[member], precise))
        orthonormal = lax.linalg.triangular_solve(
            triangle, summed[member], left_side=True, lower=True
        )
        slice_width = orthonormal.shape[1] // replicas
        own_rows = lax.dynamic_slice_in_dim(
            orthonormal, replica_index * slice_width, slice_width, 1
        )
        basis_list.append(math.sqrt(orthonormal.shape[1]) * own_rows)
        partial_rights.append(
            jnp.dot(
                orthonormal, matrices[member], precision=precise, preferred_element_type=jnp.float32
            )
        )
    between = (
        lax.psum_scatter(
            partial_rights[0].astype(jnp.bfloat16), "node", scatter_dimension=1, tiled=True
        ).astype(jnp.float32),
        lax.psum_scatter(
            partial_rights[1].astype(jnp.bfloat16), "node", scatter_dimension=1, tiled=True
        ).astype(jnp.float32),
        lax.psum_scatter(
            partial_rights[2].astype(jnp.bfloat16), "node", scatter_dimension=1, tiled=True
        ).astype(jnp.float32),
    )
    rights = (
        lax.psum_scatter(between[0], "local", scatter_dimension=1, tiled=True),
        lax.psum_scatter(between[1], "local", scatter_dimension=1, tiled=True),
        lax.psum_scatter(between[2], "local", scatter_dimension=1, tiled=True),
    )
    right_list = tuple(
        (rights[member] / (replicas * math.sqrt(matrices[member].shape[0])) for member in range(3))
    )
    return (
        leaving[None, None],
        basis_list[0][None],
        basis_list[1][None],
        basis_list[2][None],
        right_list[0][None],
        right_list[1][None],
        right_list[2][None],
    )


def solution(mesh):
    return jax.shard_map(
        local,
        mesh=mesh,
        in_specs=(
            P("section", ("node", "local"), None, None, None),
            P("section", ("node", "local"), None, None),
            P(("node", "local"), None, None, None),
            P("section", None, None),
            P("section", None, None),
            P("section", None, None),
            P("section", ("node", "local"), None, None),
            P("section", ("node", "local"), None, None),
            P("section", ("node", "local"), None, None),
            P("section", None, None),
            P("section", None, None),
            P("section", None, None),
        ),
        out_specs=(
            P("section", ("node", "local"), None, None),
            P("section", None, ("node", "local")),
            P("section", None, ("node", "local")),
            P("section", None, ("node", "local")),
            P("section", None, ("node", "local")),
            P("section", None, ("node", "local")),
            P("section", None, ("node", "local")),
        ),
        check_vma=False,
    )
```

profile of v0, /device:TPU:0, one launch (start us, length us, event | category | flops | bytes accessed | tf_op | source)
XLA Modules:
  0.0 292.2 jit_solution(3530639854416297702)
XLA Ops:
  8.1 4.7 %fusion.439 = (bf16[1,1,1,196,512]{4,2,3,1,0:T(2,128)(2,1)S(1)}, bf16[1,1,1,196,512]{4,2,3,1,0:T(2,128)(2,1)}, bf16[1,1,1,196,512]{4,2,3,1,0:T(2,128)(2,1)}, bf16[1,1,1,196,512]{4,2,3,1,0:T(2,128)(2,1)S(1)}) fusion(bf16[1,1,4,196,512]{4,2,3,1,0:T(4,128)(2,1)} %param.13), kind=kLoop, calls=%fused_computation.670 | loop fusion | bytes 1605632 | tf_op jit(solution)/shard_map/slice | solution.py:107
  18.6 1.3 collective-permute-start
  20.2 2.0 fusion.123
  42.6 1.4 copy-done.4
  44.7 1.8 constant_dynamic-update-slice_fusion.7
  46.5 1.7 constant_dynamic-update-slice_fusion.6
  48.2 1.7 constant_dynamic-update-slice_fusion.5
  49.9 1.7 constant_dynamic-update-slice_fusion.4
  51.6 1.7 constant_dynamic-update-slice_fusion.3
  59.8 1.5 collective-permute-start.1
  64.4 1.2 copy-done.7
  65.9 4.6 %collective-permute-done.1 = bf16[196,512]{1,0:T(8,128)(2,1)S(1)} collective-permute-done((bf16[196,512]{1,0:T(8,128)(2,1)S(1)}, bf16[196,512]{1,0:T(8,128)(2,1)S(1)}, u32[]{:S(2)}, u32[]{:S(2)}) %collective-permute-start.1) | collective-permute-done | bytes 200736 | tf_op jit(solution)/shard_map/ppermute | solution.py:14
  73.6 1.3 collective-permute-start.2
  77.7 1.1 copy-done.9
  79.1 2.6 collective-permute-done.2
  87.4 23.9 %psum.23 = f32[32,256]{1,0:T(8,128)S(1)} all-reduce(f32[32,256]{1,0:T(8,128)S(1)} %convolution_bitcast_fusion.2), channel_id=1, replica_groups=mesh['section'=4,'node'=4,'local'=2] {'node','local'}, use_global_device_ids=true, to_apply=%region_4.6 | all-reduce | flops 8192 | bytes 65536 | tf_op jit(solution)/shard_map/psum | solution.py:122
  111.5 2.9 cholesky.81
  115.7 2.4 custom-call.13
  135.0 3.4 %convolution_bitcast_fusion = f32[32,2304]{1,0:T(8,128)} fusion(bf16[1,1,2304,256]{3,2,1,0:T(8,128)(2,1)S(1)} %copy-done.2, f32[1,1,2304,256]{3,2,1,0:T(8,128)S(1)} %copy-done.6, f32[1,1,2304,256]{3,2,1,0:T(8,128)S(1)} %copy-done.10, f32[1,1,2304,256]{3,2,1,0:T(8,128)S(1)} %copy-done.5, f32[1,1,2304,256]{3,2,1,0:T(8,128)S(1)} %copy-done.8, ...), kind=kOutput, calls=%fused_computation | convolution fusion | flops 229441536 | bytes 10944512 | tf_op jit(solution)/shard_map/dot_general | solution.py:41
  141.8 9.6 %reduce-scatter.29.cloned.1.call-done = f32[64,32]{1,0:T(8,128)} async-done(((f32[128,32]{1,0:T(8,128)}), f32[64,32]{1,0:T(8,128)}) %reduce-scatter.29.cloned.1.call-update) | async-done | bytes 8208
  152.9 44.8 %all-reduce.39.cloned.1.call-done = (f32[32,512]{1,0:T(8,128)}, f32[32,2304]{1,0:T(8,128)}) async-done(((f32[32,512]{1,0:T(8,128)}, f32[32,2304]{1,0:T(8,128)}), (f32[32,512]{1,0:T(8,128)}, f32[32,2304]{1,0:T(8,128)})) %all-reduce.39.cloned.1.call-update) | async-done | bytes 360464 | tf_op jit(solution)/shard_map/psum | solution.py:122
  198.8 1.5 fusion.441
  200.3 2.9 %cholesky.70 = f32[32,32]{1,0:T(8,128)S(1)} custom-call(f32[32,32]{1,0:T(8,128)S(1)} %fusion.327), custom_call_target="Cholesky" | custom-call | tf_op jit(solution)/shard_map/jit(cholesky)/cholesky | solution.py:125
  204.6 2.4 custom-call.12
  207.0 1.4 fusion.325
  208.5 2.9 cholesky.59
  212.8 2.4 custom-call.11
  217.7 5.3 %fusion.48 = bf16[32,256]{1,0:T(8,128)(2,1)S(1)} fusion(f32[32,2304]{1,0:T(8,128)S(1)} %fusion.325, bf16[1,1,2304,256]{3,2,1,0:T(8,128)(2,1)S(1)} %copy-done.2, f32[2304,256]{1,0:T(8,128)} %constant_dynamic-update-slice_fusion.27, f32[2304,256]{1,0:T(8,128)} %copy-done.12, f32[2304,256]{1,0:T(8,128)} %constant_dynamic-update-slice_fusion, ...), kind=kOutput, calls=%fused_computation.98 | convolution fusion | flops 229449728 | bytes 10928128 | tf_op jit(solution)/shard_map/dot_general | solution.py:135
  224.6 12.9 %reduce-scatter.19.cloned.1.call-done = bf16[64,32]{1,0:T(8,128)(2,1)} async-done(((bf16[256,32]{1,0:T(8,128)(2,1)}), bf16[64,32]{1,0:T(8,128)(2,1)}) %reduce-scatter.19.cloned.1.call-update) | async-done | bytes 4112
  239.7 19.6 %reduce-scatter.23.cloned.1.call-done = bf16[64,32]{1,0:T(8,128)(2,1)} async-done(((bf16[256,32]{1,0:T(8,128)(2,1)}), bf16[64,32]{1,0:T(8,128)(2,1)}) %reduce-scatter.23.cloned.1.call-update) | async-done | bytes 4112
  260.8 10.5 %reduce-scatter.21.cloned.1.call-done = f32[32,32]{1,0:T(8,128)} async-done(((f32[64,32]{1,0:T(8,128)}), f32[32,32]{1,0:T(8,128)}) %reduce-scatter.21.cloned.1.call-update) | async-done | bytes 4112
  272.7 10.6 %reduce-scatter.25.cloned.1.call-done = f32[32,32]{1,0:T(8,128)} async-done(((f32[64,32]{1,0:T(8,128)}), f32[32,32]{1,0:T(8,128)}) %reduce-scatter.25.cloned.1.call-update) | async-done | bytes 4112
  (294 shorter events, 85.5 us)
Async XLA Ops:
  8.0 4.8 %copy-start = (bf16[1,512,256]{2,1,0:T(8,128)(2,1)S(1)}, bf16[1,512,256]{2,1,0:T(8,128)(2,1)}, u32[]{:S(2)}) copy-start(bf16[1,512,256]{2,1,0:T(8,128)(2,1)} %param.16) | copy-start | bytes 786436
  8.0 5.0 %copy-start.1 = (bf16[1,2304,256]{2,1,0:T(8,128)(2,1)S(1)}, bf16[1,2304,256]{2,1,0:T(8,128)(2,1)}, u32[]{:S(2)}) copy-start(bf16[1,2304,256]{2,1,0:T(8,128)(2,1)} %param.17) | copy-start | bytes 3538948
  8.0 131.1 %reduce-scatter.27.cloned.1.call-start = ((), (), s32[]{:S(2)}) async-start(), calls=%async_computation.10 | async-start | bytes 163840
  12.8 11.5 %copy-start.15 = (bf16[1,1,1,196,512]{4,2,3,1,0:T(2,128)(2,1)}, bf16[1,1,1,196,512]{4,2,3,1,0:T(2,128)(2,1)S(1)}, u32[]{:S(2)}) copy-start(bf16[1,1,1,196,512]{4,2,3,1,0:T(2,128)(2,1)S(1)} %get-tuple-element.10) | copy-start | bytes 602116
  17.3 2.9 %copy-start.27 = (bf16[1,1,196,512]{3,2,1,0:T(8,128)(2,1)S(1)}, bf16[1,1,196,512]{3,2,1,0:T(8,128)(2,1)}, u32[]{:S(2)}) copy-start(bf16[1,1,196,512]{3,2,1,0:T(8,128)(2,1)} %param.14) | copy-start | bytes 602116
  18.6 37.1 %collective-permute-start = (bf16[196,512]{1,0:T(8,128)(2,1)}, bf16[196,512]{1,0:T(8,128)(2,1)}, u32[]{:S(2)}, u32[]{:S(2)}) collective-permute-start(bf16[196,512]{1,0:T(8,128)(2,1)} %fusion.15), channel_id=1, source_target_pairs={{8,0},{16,8},{24,16},{9,1},{17,9},{25,17},{10,2},{18,10},{26,18},{... | collective-permute-start | bytes 602120 | tf_op jit(solution)/shard_map/ppermute | solution.py:14
  44.0 11.5 %copy-start.22 = (f32[196,256]{1,0:T(8,128)S(1)}, f32[196,256]{1,0:T(8,128)}, u32[]{:S(2)}) copy-start(f32[196,256]{1,0:T(8,128)} %convolution_add_fusion.23) | copy-start | bytes 602116
  44.7 8.6 %copy-start.13 = (f32[256,256]{1,0:T(8,128)S(1)}, f32[256,256]{1,0:T(8,128)}, u32[]{:S(2)}) copy-start(f32[256,256]{1,0:T(8,128)} %get-tuple-element.71) | copy-start | bytes 786436
  44.7 9.3 %copy-start.14 = (f32[256,256]{1,0:T(8,128)S(1)}, f32[256,256]{1,0:T(8,128)}, u32[]{:S(2)}) copy-start(f32[256,256]{1,0:T(8,128)} %get-tuple-element.73) | copy-start | bytes 786436
  44.7 11.0 %copy-start.23 = (bf16[1,3,196,512]{3,2,1,0:T(8,128)(2,1)S(1)}, bf16[1,3,196,512]{3,2,1,0:T(8,128)(2,1)}, u32[]{:S(2)}) copy-start(bf16[1,3,196,512]{3,2,1,0:T(8,128)(2,1)} %param.15) | copy-start | bytes 1806340
  46.5 10.2 %copy-start.34 = (bf16[1,256,512]{2,1,0:T(8,128)(2,1)S(1)}, bf16[1,256,512]{2,1,0:T(8,128)(2,1)}, u32[]{:S(2)}) copy-start(bf16[1,256,512]{2,1,0:T(8,128)(2,1)} %param.18) | copy-start | bytes 786436
  59.8 10.7 %collective-permute-start.1 = (bf16[196,512]{1,0:T(8,128)(2,1)S(1)}, bf16[196,512]{1,0:T(8,128)(2,1)S(1)}, u32[]{:S(2)}, u32[]{:S(2)}) collective-permute-start(bf16[196,512]{1,0:T(8,128)(2,1)S(1)} %add_convert_fusion.2), channel_id=1, source_target_pairs={{8,0},{16,8},{24,16},{9,1},{17,9},{25,17},{10,2},{18,10},{26,18},{... | collective-permute-start | bytes 602120 | tf_op jit(solution)/shard_map/ppermute | solution.py:14
  64.2 6.2 %copy-start.21 = (f32[196,256]{1,0:T(8,128)S(1)}, f32[196,256]{1,0:T(8,128)}, u32[]{:S(2)}) copy-start(f32[196,256]{1,0:T(8,128)} %convolution_add_fusion.14) | copy-start | bytes 602116
  65.6 4.9 %copy-start.11 = (f32[2304,256]{1,0:T(8,128)}, f32[2304,256]{1,0:T(8,128)S(1)}, u32[]{:S(2)}) copy-start(f32[2304,256]{1,0:T(8,128)S(1)} %constant_dynamic-update-slice_fusion.9) | copy-start | bytes 7077892
  73.6 8.1 %collective-permute-start.2 = (bf16[196,512]{1,0:T(8,128)(2,1)S(1)}, bf16[196,512]{1,0:T(8,128)(2,1)S(1)}, u32[]{:S(2)}, u32[]{:S(2)}) collective-permute-start(bf16[196,512]{1,0:T(8,128)(2,1)S(1)} %add_convert_fusion.1), channel_id=1, source_target_pairs={{8,0},{16,8},{24,16},{9,1},{17,9},{25,17},{10,2},{18,10},{26,18},{... | collective-permute-start | bytes 602120 | tf_op jit(solution)/shard_map/ppermute | solution.py:14
  77.5 4.2 %copy-start.28 = (f32[196,256]{1,0:T(8,128)S(1)}, f32[196,256]{1,0:T(8,128)}, u32[]{:S(2)}) copy-start(f32[196,256]{1,0:T(8,128)} %convolution_add_fusion.6) | copy-start | bytes 602116
  78.8 3.8 %copy-start.12 = (f32[2304,256]{1,0:T(8,128)}, f32[2304,256]{1,0:T(8,128)S(1)}, u32[]{:S(2)}) copy-start(f32[2304,256]{1,0:T(8,128)S(1)} %constant_dynamic-update-slice_fusion.18) | copy-start | bytes 7077892
  82.4 2.7 copy-start.35
  119.6 31.8 %reduce-scatter.29.cloned.1.call-start = ((), (), s32[]{:S(2)}) async-start(), calls=%async_computation.11 | async-start | bytes 98304
  120.7 7.9 %copy-start.16 = (bf16[1,1,1,196,512]{4,2,3,1,0:T(2,128)(2,1)S(1)}, bf16[1,1,1,196,512]{4,2,3,1,0:T(2,128)(2,1)}, u32[]{:S(2)}) copy-start(bf16[1,1,1,196,512]{4,2,3,1,0:T(2,128)(2,1)} %copy-done.15) | copy-start | bytes 602116
  121.7 13.3 %copy-start.10 = (f32[1,1,2304,256]{3,2,1,0:T(8,128)S(1)}, f32[1,1,2304,256]{3,2,1,0:T(8,128)}, u32[]{:S(2)}) copy-start(f32[1,1,2304,256]{3,2,1,0:T(8,128)} %copy-done.9) | copy-start | bytes 7077892
  123.7 5.1 %copy-start.32 = (f32[1,32,256]{2,1,0:T(8,128)S(1)}, f32[1,32,256]{2,1,0:T(8,128)}, u32[]{:S(2)}) copy-start(f32[1,32,256]{2,1,0:T(8,128)} %param.22) | copy-start | bytes 98308
  124.7 10.3 %copy-start.8 = (f32[1,1,2304,256]{3,2,1,0:T(8,128)S(1)}, f32[1,1,2304,256]{3,2,1,0:T(8,128)}, u32[]{:S(2)}) copy-start(f32[1,1,2304,256]{3,2,1,0:T(8,128)} %copy-done.7) | copy-start | bytes 7077892
  128.6 6.4 %copy-start.6 = (f32[1,1,2304,256]{3,2,1,0:T(8,128)S(1)}, f32[1,1,2304,256]{3,2,1,0:T(8,128)}, u32[]{:S(2)}) copy-start(f32[1,1,2304,256]{3,2,1,0:T(8,128)} %get-tuple-element.38) | copy-start | bytes 7077892
  128.8 6.2 %copy-start.2 = (bf16[1,1,2304,256]{3,2,1,0:T(8,128)(2,1)S(1)}, bf16[1,1,2304,256]{3,2,1,0:T(8,128)(2,1)}, u32[]{:S(2)}) copy-start(bf16[1,1,2304,256]{3,2,1,0:T(8,128)(2,1)} %param.20) | copy-start | bytes 3538948
  128.8 6.2 %copy-start.5 = (f32[1,1,2304,256]{3,2,1,0:T(8,128)S(1)}, f32[1,1,2304,256]{3,2,1,0:T(8,128)}, u32[]{:S(2)}) copy-start(f32[1,1,2304,256]{3,2,1,0:T(8,128)} %copy-done.4) | copy-start | bytes 7077892
  128.9 6.2 %copy-start.31 = (f32[1,32,256]{2,1,0:T(8,128)S(1)}, f32[1,32,256]{2,1,0:T(8,128)}, u32[]{:S(2)}) copy-start(f32[1,32,256]{2,1,0:T(8,128)} %param.23) | copy-start | bytes 98308
  140.8 56.9 %all-reduce.39.cloned.1.call-start = ((), (), s32[]{:S(2)}) async-start(), calls=%async_computation.12 | async-start | bytes 720896 | tf_op jit(solution)/shard_map/psum | solution.py:122
  141.5 95.9 %reduce-scatter.19.cloned.1.call-start = ((), (), s32[]{:S(2)}) async-start(), calls=%async_computation.6 | async-start | bytes 81920
  217.7 41.6 %reduce-scatter.23.cloned.1.call-start = ((), (), s32[]{:S(2)}) async-start(), calls=%async_computation.8 | async-start | bytes 81920
  223.8 47.5 %reduce-scatter.21.cloned.1.call-start = ((), (), s32[]{:S(2)}) async-start(), calls=%async_computation.7 | async-start | bytes 49152
  238.9 44.4 %reduce-scatter.25.cloned.1.call-start = ((), (), s32[]{:S(2)}) async-start(), calls=%async_computation.9 | async-start | bytes 49152
  (16 other events, 29.9 us)
Sparse Core Ops, SparseCore 0:
  119.7 19.3 reduce-scatter.26
  141.3 10.0 reduce-scatter.28
  217.8 19.5 reduce-scatter.18
  239.7 19.5 reduce-scatter.22
  261.3 9.9 reduce-scatter.20
  273.4 9.9 reduce-scatter.24
Sparse Core Ops, SparseCore 1:
  144.4 53.2 all-reduce.38
where the time goes:
time: 293 us; the launch traced here: 292 us
  waiting for transfers between devices  115 us (39%)
  matrix products  68.9 us (24%)
  local copies, waits for them, and re-layouts  37.5 us (13%)
  other arithmetic  25 us (9%)
  blocking collectives  23.9 us (8%)
  between operations  16.9 us (6%)
  starting transfers between devices  4.56 us (2%)
    unnamed x13, waiting for transfers between devices  63.4 us
    psum x1, waiting for transfers between devices, local(): summed = lax.psum((factors[0], factors[1], factors[2]), ('node', 'local'))  44.8 us
    unnamed x121, local copies, waits for them, and re-layouts  31.1 us
    dot_general x44, matrix products, inner_rows(): lax.dot_general(left_operand, right_operand, (((0,), (0,)), ((), ())), pr...  27 us
    psum x1, blocking collectives, local(): summed = lax.psum((factors[0], factors[1], factors[2]), ('node', 'local'))  23.9 us
    dot_general x50, matrix products, inner_cols(): lax.dot_general(left_operand, right_operand, (((1,), (1,)), ((), ())), pr...  19.7 us
    another operation x9, other arithmetic, local(): jnp.linalg.cholesky(inner_cols(summed[member], summed[member], precise))  10.8 us
    dot_general x36, matrix products, block_backward(): jnp.dot(moved, spatial_weight[tap * channels:(tap + 1) * channels], prefe...  10.2 us
  transfers between devices with their start and end apart: 10, of which 8 were waited for; matrix products, arithmetic and copies ran while one was open for 25% of the time, Pallas kernels for 0%

commit v1 on v0

--- a/solution.py
+++ b/solution.py
@@ -119,7 +119,8 @@
     replicas = lax.axis_size(("node", "local"))
     replica_index = lax.axis_index(("node", "local"))
     basis_list = []
-    summed = lax.psum((factors[0], factors[1], factors[2]), ("node", "local"))
+    half = lax.psum((factors[0], factors[1], factors[2]), "local")
+    summed = lax.psum(half, "node")
     partial_rights = []
     for member in range(3):
         triangle = jnp.linalg.cholesky(inner_cols(summed[member], summed[member], precise))

time: 293 us -> 305 us (1.041)
  waiting for transfers between devices: 115 us -> 130 us
  blocking collectives: 23.9 us -> 18.5 us
  matrix products: 68.9 us -> 74.1 us
    psum x1 -> x2, waiting for transfers between devices: 44.8 us -> 61 us  [the longest x1 34.3 us: local(): summed = lax.psum(half, 'node')]
    dot_general x50, matrix products: 19.7 us -> 25.2 us  [inner_cols(): lax.dot_general(left_operand, right_operand, (((1,), (1,)), ((), ())), pr...]
    psum x1 -> x2, blocking collectives: 23.9 us -> 18.5 us  [the longest x1 10.3 us: local(): summed = lax.psum(half, 'node')]
    unnamed x13 -> x14, waiting for transfers between devices: 63.4 us -> 61.9 us
    unnamed x121 -> x151, local copies, waits for them, and re-layouts: 31.1 us -> 30.2 us
  transfers between devices with their start and end apart: 10 -> 11, of which waited for: 8 -> 10; matrix products, arithmetic and copies ran while one was open for 25% -> 24% of each run, Pallas kernels for 0% -> 0%
where the time goes in v1:
time: 305 us; the launch traced here: 304 us
  waiting for transfers between devices  130 us (43%)
  matrix products  74.1 us (24%)
  local copies, waits for them, and re-layouts  36.5 us (12%)
  other arithmetic  25 us (8%)
  blocking collectives  18.5 us (6%)
  between operations  15.6 us (5%)
  starting transfers between devices  4.59 us (2%)
    unnamed x14, waiting for transfers between devices  61.9 us
    psum x1, waiting for transfers between devices, local(): summed = lax.psum(half, 'node')  34.3 us
    unnamed x151, local copies, waits for them, and re-layouts  30.2 us
    psum x1, waiting for transfers between devices, local(): half = lax.psum((factors[0], factors[1], factors[2]), 'local')  26.6 us
    dot_general x44, matrix products, inner_rows(): lax.dot_general(left_operand, right_operand, (((0,), (0,)), ((), ())), pr...  26.3 us
    dot_general x50, matrix products, inner_cols(): lax.dot_general(left_operand, right_operand, (((1,), (1,)), ((), ())), pr...  25.2 us
    another operation x9, other arithmetic, local(): jnp.linalg.cholesky(inner_cols(summed[member], summed[member], precise))  10.8 us
    psum x1, blocking collectives, local(): summed = lax.psum(half, 'node')  10.3 us
  transfers between devices with their start and end apart: 11, of which 10 were waited for; matrix products, arithmetic and copies ran while one was open for 24% of the time, Pallas kernels for 0%

profile of v1, /device:TPU:0, one launch (start us, length us, event | category | flops | bytes accessed | tf_op | source)
XLA Modules:
  0.0 304.4 jit_solution(2854002450172380678)
XLA Ops:
  7.3 4.6 %fusion.439 = (bf16[1,1,1,196,512]{4,2,3,1,0:T(2,128)(2,1)}, bf16[1,1,1,196,512]{4,2,3,1,0:T(2,128)(2,1)}, bf16[1,1,1,196,512]{4,2,3,1,0:T(2,128)(2,1)}, bf16[1,1,1,196,512]{4,2,3,1,0:T(2,128)(2,1)S(1)}) fusion(bf16[1,1,4,196,512]{4,2,3,1,0:T(4,128)(2,1)} %param.13), kind=kLoop, calls=%fused_computation.670 | loop fusion | bytes 1605632 | tf_op jit(solution)/shard_map/slice | solution.py:107
  17.7 1.3 collective-permute-start
  21.6 1.9 multiply_convert_fusion.4
  40.1 1.4 copy-done.4
  42.3 1.8 constant_dynamic-update-slice_fusion.7
  44.0 1.7 constant_dynamic-update-slice_fusion.6
  45.8 1.7 constant_dynamic-update-slice_fusion.5
  47.5 1.7 constant_dynamic-update-slice_fusion.4
  49.1 1.7 constant_dynamic-update-slice_fusion.3
  57.3 1.5 collective-permute-start.1
  63.3 4.6 %collective-permute-done.1 = bf16[196,512]{1,0:T(8,128)(2,1)S(1)} collective-permute-done((bf16[196,512]{1,0:T(8,128)(2,1)S(1)}, bf16[196,512]{1,0:T(8,128)(2,1)S(1)}, u32[]{:S(2)}, u32[]{:S(2)}) %collective-permute-start.1) | collective-permute-done | bytes 200736 | tf_op jit(solution)/shard_map/ppermute | solution.py:14
  71.1 1.3 collective-permute-start.2
  76.6 2.6 collective-permute-done.2
  89.1 8.2 %psum.46 = f32[32,256]{1,0:T(8,128)S(1)} all-reduce(f32[32,256]{1,0:T(8,128)S(1)} %convolution_bitcast_fusion.2), channel_id=1, replica_groups=mesh['section'=4,'node'=4,'local'=2] {'local'}, use_global_device_ids=true, to_apply=%region_6.8 | all-reduce | flops 8192 | bytes 65536 | tf_op jit(solution)/shard_map/psum | solution.py:122
  97.3 10.3 %psum.47 = f32[32,256]{1,0:T(8,128)S(1)} all-reduce(f32[32,256]{1,0:T(8,128)S(1)} %psum.46), channel_id=1, replica_groups=mesh['section'=4,'node'=4,'local'=2] {'node'}, use_global_device_ids=true, to_apply=%region_7.9 | all-reduce | flops 8192 | bytes 65536 | tf_op jit(solution)/shard_map/psum | solution.py:123
  107.8 2.9 cholesky.81
  112.1 2.4 custom-call.13
  130.7 3.3 %convolution_bitcast_fusion = f32[32,2304]{1,0:T(8,128)} fusion(bf16[1,1,2304,256]{3,2,1,0:T(8,128)(2,1)S(1)} %copy-done.2, f32[1,1,2304,256]{3,2,1,0:T(8,128)S(1)} %copy-done.6, f32[1,1,2304,256]{3,2,1,0:T(8,128)S(1)} %copy-done.10, f32[1,1,2304,256]{3,2,1,0:T(8,128)S(1)} %copy-done.5, f32[1,1,2304,256]{3,2,1,0:T(8,128)S(1)} %copy-done.8, ...), kind=kOutput, calls=%fused_computation | convolution fusion | flops 229441536 | bytes 10944512 | tf_op jit(solution)/shard_map/dot_general | solution.py:41
  140.5 7.2 %reduce-scatter.29.cloned.1.call-done = f32[64,32]{1,0:T(8,128)} async-done(((f32[128,32]{1,0:T(8,128)}), f32[64,32]{1,0:T(8,128)}) %reduce-scatter.29.cloned.1.call-update) | async-done | bytes 8208
  148.5 26.6 %all-reduce.43.cloned.1.call-done = (f32[32,512]{1,0:T(8,128)}, f32[32,2304]{1,0:T(8,128)}) async-done(((f32[32,512]{1,0:T(8,128)}, f32[32,2304]{1,0:T(8,128)}), (f32[32,512]{1,0:T(8,128)}, f32[32,2304]{1,0:T(8,128)})) %all-reduce.43.cloned.1.call-update) | async-done | bytes 360464 | tf_op jit(solution)/shard_map/psum | solution.py:122
  175.9 34.3 %all-reduce.41.cloned.1.call-done = (f32[32,512]{1,0:T(8,128)}, f32[32,2304]{1,0:T(8,128)}) async-done(((f32[32,512]{1,0:T(8,128)}, f32[32,2304]{1,0:T(8,128)}), (f32[32,512]{1,0:T(8,128)}, f32[32,2304]{1,0:T(8,128)})) %all-reduce.41.cloned.1.call-update) | async-done | bytes 360464 | tf_op jit(solution)/shard_map/psum | solution.py:123
  211.3 1.5 fusion.441
  212.9 2.9 cholesky.70
  217.1 2.4 custom-call.12
  219.5 1.4 fusion.325
  221.1 2.9 cholesky.59
  225.3 2.4 custom-call.11
  230.2 5.3 %fusion.48 = bf16[32,256]{1,0:T(8,128)(2,1)S(1)} fusion(f32[32,2304]{1,0:T(8,128)S(1)} %fusion.325, bf16[1,1,2304,256]{3,2,1,0:T(8,128)(2,1)S(1)} %copy-done.2, f32[2304,256]{1,0:T(8,128)} %constant_dynamic-update-slice_fusion.27, f32[2304,256]{1,0:T(8,128)} %copy-done.12, f32[2304,256]{1,0:T(8,128)} %constant_dynamic-update-slice_fusion, ...), kind=kOutput, calls=%fused_computation.98 | convolution fusion | flops 229449728 | bytes 10928128 | tf_op jit(solution)/shard_map/dot_general | solution.py:136
  237.1 12.8 %reduce-scatter.19.cloned.1.call-done = bf16[64,32]{1,0:T(8,128)(2,1)} async-done(((bf16[256,32]{1,0:T(8,128)(2,1)}), bf16[64,32]{1,0:T(8,128)(2,1)}) %reduce-scatter.19.cloned.1.call-update) | async-done | bytes 4112
  252.2 19.6 %reduce-scatter.23.cloned.1.call-done = bf16[64,32]{1,0:T(8,128)(2,1)} async-done(((bf16[256,32]{1,0:T(8,128)(2,1)}), bf16[64,32]{1,0:T(8,128)(2,1)}) %reduce-scatter.23.cloned.1.call-update) | async-done | bytes 4112
  273.3 10.7 %reduce-scatter.21.cloned.1.call-done = f32[32,32]{1,0:T(8,128)} async-done(((f32[64,32]{1,0:T(8,128)}), f32[32,32]{1,0:T(8,128)}) %reduce-scatter.21.cloned.1.call-update) | async-done | bytes 4112
  285.3 10.8 %reduce-scatter.25.cloned.1.call-done = f32[32,32]{1,0:T(8,128)} async-done(((f32[64,32]{1,0:T(8,128)}), f32[32,32]{1,0:T(8,128)}) %reduce-scatter.25.cloned.1.call-update) | async-done | bytes 4112
  (328 shorter events, 93.0 us)
Async XLA Ops:
  7.2 128.3 %reduce-scatter.27.cloned.1.call-start = ((), (), s32[]{:S(2)}) async-start(), calls=%async_computation.10 | async-start | bytes 163840
  17.7 35.5 %collective-permute-start = (bf16[196,512]{1,0:T(8,128)(2,1)}, bf16[196,512]{1,0:T(8,128)(2,1)}, u32[]{:S(2)}, u32[]{:S(2)}) collective-permute-start(bf16[196,512]{1,0:T(8,128)(2,1)} %fusion.15), channel_id=1, source_target_pairs={{8,0},{16,8},{24,16},{9,1},{17,9},{25,17},{10,2},{18,10},{26,18},{... | collective-permute-start | bytes 602120 | tf_op jit(solution)/shard_map/ppermute | solution.py:14
  29.2 38.8 %copy-start.22 = (f32[196,256]{1,0:T(8,128)}, f32[196,256]{1,0:T(8,128)S(1)}, u32[]{:S(2)}) copy-start(f32[196,256]{1,0:T(8,128)S(1)} %convolution_add_fusion.14) | copy-start | bytes 602116
  41.5 11.5 %copy-start.24 = (f32[196,256]{1,0:T(8,128)S(1)}, f32[196,256]{1,0:T(8,128)}, u32[]{:S(2)}) copy-start(f32[196,256]{1,0:T(8,128)} %convolution_add_fusion.23) | copy-start | bytes 602116
  42.3 8.5 %copy-start.15 = (f32[256,256]{1,0:T(8,128)S(1)}, f32[256,256]{1,0:T(8,128)}, u32[]{:S(2)}) copy-start(f32[256,256]{1,0:T(8,128)} %get-tuple-element.73) | copy-start | bytes 786436
  42.3 9.3 %copy-start.16 = (f32[256,256]{1,0:T(8,128)S(1)}, f32[256,256]{1,0:T(8,128)}, u32[]{:S(2)}) copy-start(f32[256,256]{1,0:T(8,128)} %get-tuple-element.75) | copy-start | bytes 786436
  42.3 11.0 %copy-start.27 = (bf16[1,3,196,512]{3,2,1,0:T(8,128)(2,1)S(1)}, bf16[1,3,196,512]{3,2,1,0:T(8,128)(2,1)}, u32[]{:S(2)}) copy-start(bf16[1,3,196,512]{3,2,1,0:T(8,128)(2,1)} %param.15) | copy-start | bytes 1806340
  44.0 10.2 %copy-start.49 = (bf16[1,256,512]{2,1,0:T(8,128)(2,1)S(1)}, bf16[1,256,512]{2,1,0:T(8,128)(2,1)}, u32[]{:S(2)}) copy-start(bf16[1,256,512]{2,1,0:T(8,128)(2,1)} %param.18) | copy-start | bytes 786436
  57.3 10.7 %collective-permute-start.1 = (bf16[196,512]{1,0:T(8,128)(2,1)S(1)}, bf16[196,512]{1,0:T(8,128)(2,1)S(1)}, u32[]{:S(2)}, u32[]{:S(2)}) collective-permute-start(bf16[196,512]{1,0:T(8,128)(2,1)S(1)} %add_convert_fusion.2), channel_id=1, source_target_pairs={{8,0},{16,8},{24,16},{9,1},{17,9},{25,17},{10,2},{18,10},{26,18},{... | collective-permute-start | bytes 602120 | tf_op jit(solution)/shard_map/ppermute | solution.py:14
  71.1 8.1 %collective-permute-start.2 = (bf16[196,512]{1,0:T(8,128)(2,1)S(1)}, bf16[196,512]{1,0:T(8,128)(2,1)S(1)}, u32[]{:S(2)}, u32[]{:S(2)}) collective-permute-start(bf16[196,512]{1,0:T(8,128)(2,1)S(1)} %add_convert_fusion.1), channel_id=1, source_target_pairs={{8,0},{16,8},{24,16},{9,1},{17,9},{25,17},{10,2},{18,10},{26,18},{... | collective-permute-start | bytes 602120 | tf_op jit(solution)/shard_map/ppermute | solution.py:14
  79.2 7.5 %copy-start.25 = (bf16[196,512]{1,0:T(8,128)(2,1)}, bf16[196,512]{1,0:T(8,128)(2,1)S(1)}, u32[]{:S(2)}) copy-start(bf16[196,512]{1,0:T(8,128)(2,1)S(1)} %bitcast_select_fusion.2) | copy-start | bytes 602116
  81.3 6.8 %copy-start.31 = (bf16[1,1,256,512]{3,2,1,0:T(8,128)(2,1)S(1)}, bf16[1,1,256,512]{3,2,1,0:T(8,128)(2,1)}, u32[]{:S(2)}) copy-start(bf16[1,1,256,512]{3,2,1,0:T(8,128)(2,1)} %param.21) | copy-start | bytes 786436
  116.0 31.7 %reduce-scatter.29.cloned.1.call-start = ((), (), s32[]{:S(2)}) async-start(), calls=%async_computation.11 | async-start | bytes 98304
  118.1 7.0 %copy-start.37 = (f32[196,256]{1,0:T(8,128)S(1)}, f32[196,256]{1,0:T(8,128)}, u32[]{:S(2)}) copy-start(f32[196,256]{1,0:T(8,128)} %fusion.126) | copy-start | bytes 602116
  118.1 7.0 %copy-start.38 = (f32[196,256]{1,0:T(8,128)S(1)}, f32[196,256]{1,0:T(8,128)}, u32[]{:S(2)}) copy-start(f32[196,256]{1,0:T(8,128)} %fusion.138) | copy-start | bytes 602116
  118.1 7.0 %copy-start.39 = (f32[196,256]{1,0:T(8,128)S(1)}, f32[196,256]{1,0:T(8,128)}, u32[]{:S(2)}) copy-start(f32[196,256]{1,0:T(8,128)} %fusion.150) | copy-start | bytes 602116
  118.1 7.0 %copy-start.40 = (f32[196,256]{1,0:T(8,128)S(1)}, f32[196,256]{1,0:T(8,128)}, u32[]{:S(2)}) copy-start(f32[196,256]{1,0:T(8,128)} %fusion.162) | copy-start | bytes 602116
  118.1 7.0 %copy-start.41 = (f32[196,256]{1,0:T(8,128)S(1)}, f32[196,256]{1,0:T(8,128)}, u32[]{:S(2)}) copy-start(f32[196,256]{1,0:T(8,128)} %fusion.182) | copy-start | bytes 602116
  118.1 7.0 %copy-start.42 = (f32[196,256]{1,0:T(8,128)S(1)}, f32[196,256]{1,0:T(8,128)}, u32[]{:S(2)}) copy-start(f32[196,256]{1,0:T(8,128)} %fusion.194) | copy-start | bytes 602116
  118.1 7.0 %copy-start.43 = (f32[196,256]{1,0:T(8,128)S(1)}, f32[196,256]{1,0:T(8,128)}, u32[]{:S(2)}) copy-start(f32[196,256]{1,0:T(8,128)} %fusion.206) | copy-start | bytes 602116
  118.1 7.0 %copy-start.44 = (f32[196,256]{1,0:T(8,128)S(1)}, f32[196,256]{1,0:T(8,128)}, u32[]{:S(2)}) copy-start(f32[196,256]{1,0:T(8,128)} %fusion.218) | copy-start | bytes 602116
  118.1 7.0 %copy-start.50 = (f32[196,256]{1,0:T(8,128)S(1)}, f32[196,256]{1,0:T(8,128)}, u32[]{:S(2)}) copy-start(f32[196,256]{1,0:T(8,128)} %get-tuple-element.23) | copy-start | bytes 602116
  120.2 10.4 %copy-start.46 = (f32[1,32,256]{2,1,0:T(8,128)S(1)}, f32[1,32,256]{2,1,0:T(8,128)}, u32[]{:S(2)}) copy-start(f32[1,32,256]{2,1,0:T(8,128)} %param.23) | copy-start | bytes 98308
  121.2 9.4 %copy-start.10 = (f32[1,1,2304,256]{3,2,1,0:T(8,128)S(1)}, f32[1,1,2304,256]{3,2,1,0:T(8,128)}, u32[]{:S(2)}) copy-start(f32[1,1,2304,256]{3,2,1,0:T(8,128)} %copy-done.9) | copy-start | bytes 7077892
  130.7 8.9 %copy-start.26 = (bf16[196,512]{1,0:T(8,128)(2,1)S(1)}, bf16[196,512]{1,0:T(8,128)(2,1)}, u32[]{:S(2)}) copy-start(bf16[196,512]{1,0:T(8,128)(2,1)} %copy-done.25) | copy-start | bytes 602116
  130.7 8.9 %copy-start.30 = (bf16[196,256]{1,0:T(8,128)(2,1)S(1)}, bf16[196,256]{1,0:T(8,128)(2,1)}, u32[]{:S(2)}) copy-start(bf16[196,256]{1,0:T(8,128)(2,1)} %copy-done.29) | copy-start | bytes 301060
  137.1 38.1 %all-reduce.43.cloned.1.call-start = ((), (), s32[]{:S(2)}) async-start(), calls=%async_computation.13 | async-start | bytes 720896 | tf_op jit(solution)/shard_map/psum | solution.py:122
  137.9 72.3 %all-reduce.41.cloned.1.call-start = ((), (), s32[]{:S(2)}) async-start(), calls=%async_computation.12 | async-start | bytes 720896 | tf_op jit(solution)/shard_map/psum | solution.py:123
  175.2 74.7 %reduce-scatter.19.cloned.1.call-start = ((), (), s32[]{:S(2)}) async-start(), calls=%async_computation.6 | async-start | bytes 81920
  230.2 41.6 %reduce-scatter.23.cloned.1.call-start = ((), (), s32[]{:S(2)}) async-start(), calls=%async_computation.8 | async-start | bytes 81920
  236.3 47.6 %reduce-scatter.21.cloned.1.call-start = ((), (), s32[]{:S(2)}) async-start(), calls=%async_computation.7 | async-start | bytes 49152
  251.4 44.7 %reduce-scatter.25.cloned.1.call-start = ((), (), s32[]{:S(2)}) async-start(), calls=%async_computation.9 | async-start | bytes 49152
  (32 other events, 111.9 us)
Sparse Core Ops, SparseCore 0:
  116.1 19.3 reduce-scatter.26
  137.7 10.0 reduce-scatter.28
  150.0 25.0 all-reduce.42
  177.4 32.7 all-reduce.40
  230.3 19.5 reduce-scatter.18
  252.2 19.5 reduce-scatter.22
  273.9 9.9 reduce-scatter.20
  286.1 9.9 reduce-scatter.24
